TPU v7x, 32 devices: a whole 2x2x4 slice. The times are simulated.
32 devices in a mesh: grp: 1, row: 32 (over z, y, x, core).
Axes of the slice: x: 2, y: 2, z: 4, core: 2. Of those that a mesh axis runs over, the one named last changes fastest.
Arguments:
- homolog_matrix: bfloat16 [64, 128, 256], P(('grp', 'row')), may hold values from -6 to 6
- alignment_mask: int32 [64, 128], P(('grp', 'row')), may hold values from 0 to 1, as said below
- pair_state_input: bfloat16 [128, 128, 128], P(('grp', 'row')), may hold values from -3 to 3
- chain_label: int32 [128], P('grp'), may hold values from 0 to 3, never falling along the last dimension, each value on 1 to 64 neighbouring positions
- residue_number_index: int32 [128], P('grp'), may hold values from 1 to 382, as said below
- relative_position_table: float32 [66, 128], replicated, may hold values from -3 to 3
- tensor_factor_coefficients: bfloat16 [256, 64], replicated, may hold values from -0.375 to 0.375
- outer_output_weight: bfloat16 [1024, 128], replicated, may hold values from -3 to 3
- scorer_entry_coefficients: bfloat16 [256, 1024], replicated, may hold values from -0.375 to 0.375
- scorer_final_coefficients: bfloat16 [256, 256], replicated, may hold values from -0.375 to 0.375
- pair_bias_weight: bfloat16 [128, 8], replicated
- triangle_input_weight: bfloat16 [128, 512], replicated, may hold values from -0.5 to 0.5
- triangle_output_gate: bfloat16 [128, 128], replicated, may hold values from -1.5 to 1.5
- triangle_output_weight: bfloat16 [128, 128], replicated, may hold values from -1.796875 to 1.796875
Outputs:
- homolog_revised: bfloat16 [64, 128, 256], P(('grp', 'row'))
- pair_state_output: bfloat16 [128, 128, 128], P(('grp', 'row'))
Inputs may be any that keep to these rules, and one draw needn't show every extreme that they name: `alignment_mask`: 1 marks a live entry of an MSA row. `chain_label`: chain ids never fall along the residues; a chain holds at most 64 residues. `residue_number_index`: residue numbers strictly increase along the residues.
All inputs are finite; a program needn't handle non-finite values.
Results may differ from a plain program's by a relative error of at most 0.03.
Values may be sent and summed in bfloat16 or wider, within the bound.
A program may use at most 128 MiB of HBM per device.

v0:
```python
import jax
import jax.numpy as jnp
from jax import lax
from jax.sharding import PartitionSpec as P

REL_MAX = 32


def layer_normalize(values):
    centre = jnp.mean(values, axis=-1, keepdims=True)
    shifted = values - centre
    spread = jnp.mean(shifted * shifted, axis=-1, keepdims=True)
    return shifted * lax.rsqrt(spread + 1e-05)


def on_device(
    homolog_matrix,
    alignment_mask,
    pair_state_input,
    chain_label,
    residue_number_index,
    relative_position_table,
    tensor_factor_coefficients,
    outer_output_weight,
    scorer_entry_coefficients,
    scorer_final_coefficients,
    pair_bias_weight,
    triangle_input_weight,
    triangle_output_gate,
    triangle_output_weight,
):
    sequence_local_rows = homolog_matrix.shape[0]
    residue_total = homolog_matrix.shape[1]
    alignment_width = homolog_matrix.shape[2]
    res_local = pair_state_input.shape[0]
    pair_width = pair_state_input.shape[2]
    opm_width = tensor_factor_coefficients.shape[1] // 2
    head_total = pair_bias_weight.shape[1]
    head_channel_width = alignment_width // head_total
    tri_width = triangle_input_weight.shape[1] // 4
    table_rows = relative_position_table.shape[0]
    row_start = lax.axis_index("row") * res_local
    contract = (((0,), (0,)), ((), ()))
    active_entry_mask = alignment_mask.astype(jnp.float32)
    homolog_rescaled = layer_normalize(homolog_matrix.astype(jnp.float32)).astype(jnp.bfloat16)
    homolog_lines_merged = homolog_rescaled.reshape(
        sequence_local_rows * residue_total, alignment_width
    )
    projected_rows = jnp.dot(
        homolog_lines_merged, tensor_factor_coefficients, preferred_element_type=jnp.float32
    ).reshape(sequence_local_rows, residue_total, 2 * opm_width)
    left_factor = (
        (projected_rows[..., :opm_width] * active_entry_mask[..., None])
        .astype(jnp.bfloat16)
        .reshape(sequence_local_rows, residue_total * opm_width)
    )
    right_factor = (
        (projected_rows[..., opm_width:] * active_entry_mask[..., None])
        .astype(jnp.bfloat16)
        .reshape(sequence_local_rows, residue_total * opm_width)
    )
    live_weights = active_entry_mask.astype(jnp.bfloat16)
    left_all, right_all, live_all = (
        lax.all_gather(left_factor, "row", axis=0, tiled=True),
        lax.all_gather(right_factor, "row", axis=0, tiled=True),
        lax.all_gather(live_weights, "row", axis=0, tiled=True),
    )
    left_cols = lax.dynamic_slice_in_dim(left_all, row_start * opm_width, res_local * opm_width, 1)
    live_cols = lax.dynamic_slice_in_dim(live_all, row_start, res_local, 1)
    outer_sum = lax.dot_general(left_cols, right_all, contract, preferred_element_type=jnp.float32)
    pair_count = lax.dot_general(live_cols, live_all, contract, preferred_element_type=jnp.float32)
    outer_flat = outer_sum.reshape(res_local, opm_width, residue_total, opm_width).transpose(
        0, 2, 1, 3
    )
    outer_flat = outer_flat.reshape(res_local * residue_total, opm_width * opm_width).astype(
        jnp.bfloat16
    )
    opm_update = jnp.dot(
        outer_flat, outer_output_weight, preferred_element_type=jnp.float32
    ).reshape(res_local, residue_total, pair_width)
    opm_update = opm_update / (0.001 + pair_count[..., None])
    chain_rows = lax.dynamic_slice_in_dim(chain_label, row_start, res_local, 0)
    index_rows = lax.dynamic_slice_in_dim(residue_number_index, row_start, res_local, 0)
    same_chain = chain_rows[:, None] == chain_label[None, :]
    offsets = (
        jnp.clip(index_rows[:, None] - residue_number_index[None, :], -REL_MAX, REL_MAX) + REL_MAX
    )
    bin_index = jnp.where(same_chain, offsets, 2 * REL_MAX + 1)
    one_hot = (
        (bin_index[..., None] == jnp.arange(table_rows, dtype=jnp.int32))
        .astype(jnp.float32)
        .reshape(-1, table_rows)
    )
    position_term = jnp.dot(
        one_hot, relative_position_table, precision=lax.Precision.HIGHEST
    ).reshape(res_local, residue_total, pair_width)
    updated = (pair_state_input.astype(jnp.float32) + position_term + opm_update).astype(
        jnp.bfloat16
    )
    pair_norm = layer_normalize(updated.astype(jnp.float32)).astype(jnp.bfloat16)
    pair_flat = pair_norm.reshape(res_local * residue_total, pair_width)
    head_bias = jnp.dot(pair_flat, pair_bias_weight, preferred_element_type=jnp.float32).astype(
        jnp.bfloat16
    )
    head_bias = head_bias.reshape(res_local, residue_total, head_total).transpose(2, 0, 1)
    full_bias = lax.all_gather(head_bias, "row", axis=1, tiled=True)
    tri_projected = jnp.dot(pair_flat, triangle_input_weight, preferred_element_type=jnp.float32)
    tri_left = (
        jax.nn.sigmoid(tri_projected[:, :tri_width]) * tri_projected[:, tri_width : 2 * tri_width]
    ).astype(jnp.bfloat16)
    tri_right = (
        jax.nn.sigmoid(tri_projected[:, 2 * tri_width : 3 * tri_width])
        * tri_projected[:, 3 * tri_width :]
    ).astype(jnp.bfloat16)
    tri_left = tri_left.reshape(res_local, residue_total, tri_width).transpose(2, 0, 1)
    tri_right = tri_right.reshape(res_local, residue_total, tri_width).transpose(2, 0, 1)
    left_channels, right_channels = (
        lax.all_to_all(tri_left, "row", split_axis=0, concat_axis=1, tiled=True),
        lax.all_to_all(tri_right, "row", split_axis=0, concat_axis=1, tiled=True),
    )
    channel_sum = jnp.einsum(
        "cki,ckj->cij", left_channels, right_channels, preferred_element_type=jnp.float32
    ).astype(jnp.bfloat16)
    row_sum = lax.all_to_all(channel_sum, "row", split_axis=1, concat_axis=0, tiled=True)
    tri_sum = row_sum.transpose(1, 2, 0)
    tri_normed = (
        layer_normalize(tri_sum.astype(jnp.float32))
        .astype(jnp.bfloat16)
        .reshape(res_local * residue_total, tri_width)
    )
    tri_gating = jax.nn.sigmoid(
        jnp.dot(pair_flat, triangle_output_gate, preferred_element_type=jnp.float32)
    )
    pair_state_output = updated.astype(jnp.float32).reshape(
        res_local * residue_total, pair_width
    ) + tri_gating * jnp.dot(tri_normed, triangle_output_weight, preferred_element_type=jnp.float32)
    pair_state_output = pair_state_output.astype(jnp.bfloat16).reshape(
        res_local, residue_total, pair_width
    )
    scorer_mapped_lines = jnp.dot(
        homolog_lines_merged, scorer_entry_coefficients, preferred_element_type=jnp.float32
    )
    asking_vectors = (
        scorer_mapped_lines[:, :alignment_width]
        .astype(jnp.bfloat16)
        .reshape(sequence_local_rows, residue_total, head_total, head_channel_width)
    )
    lookup_lines = (
        scorer_mapped_lines[:, alignment_width : 2 * alignment_width]
        .astype(jnp.bfloat16)
        .reshape(sequence_local_rows, residue_total, head_total, head_channel_width)
    )
    content_lines = (
        scorer_mapped_lines[:, 2 * alignment_width : 3 * alignment_width]
        .astype(jnp.bfloat16)
        .reshape(sequence_local_rows, residue_total, head_total, head_channel_width)
    )
    sigmoid_factor = (
        scorer_mapped_lines[:, 3 * alignment_width :]
        .astype(jnp.bfloat16)
        .reshape(sequence_local_rows, residue_total, head_total, head_channel_width)
    )
    mask_term = 1000000000.0 * (active_entry_mask - 1.0)
    score_scale = head_channel_width ** (-0.5)

    def attend(row_inputs):
        query_row, key_row, value_row, gate_row, mask_row = row_inputs
        scores = (
            jnp.einsum("ihd,jhd->hij", query_row, key_row, preferred_element_type=jnp.float32)
            * score_scale
        )
        scores = scores + full_bias.astype(jnp.float32) + mask_row[None, None, :]
        weights = jax.nn.softmax(scores, axis=-1).astype(jnp.bfloat16)
        attended = jnp.einsum(
            "hij,jhd->ihd", weights, value_row, preferred_element_type=jnp.float32
        )
        return (jax.nn.sigmoid(gate_row.astype(jnp.float32)) * attended).astype(jnp.bfloat16)

    sigmoid_scaled_lines = lax.map(
        attend, (asking_vectors, lookup_lines, content_lines, sigmoid_factor, mask_term)
    )
    homolog_revised = homolog_matrix.astype(jnp.float32).reshape(
        sequence_local_rows * residue_total, alignment_width
    ) + jnp.dot(
        sigmoid_scaled_lines.reshape(sequence_local_rows * residue_total, alignment_width),
        scorer_final_coefficients,
        preferred_element_type=jnp.float32,
    )
    homolog_revised = homolog_revised.astype(jnp.bfloat16).reshape(
        sequence_local_rows, residue_total, alignment_width
    )
    return (homolog_revised, pair_state_output)


def solution(mesh):
    return jax.shard_map(
        on_device,
        mesh=mesh,
        in_specs=(
            P(("grp", "row"), None, None),
            P(("grp", "row"), None),
            P(("grp", "row"), None, None),
            P("grp"),
            P("grp"),
            P(),
            P(),
            P(),
            P(),
            P(),
            P(),
            P(),
            P(),
            P(),
        ),
        out_specs=(P(("grp", "row"), None, None), P(("grp", "row"), None, None)),
        check_vma=False,
    )
```

profile of v0, /device:TPU:0, one launch (start us, length us, event | category | flops | bytes accessed | tf_op | source)
XLA Modules:
  0.0 210.1 jit_solution(4078920670390650498)
XLA Ops:
  0.6 1.1 convert_reduce_fusion
  1.7 1.1 multiply_reduce_fusion.2
  2.8 1.0 multiply_convert_fusion.2
  3.9 0.7 convert_bitcast_fusion
  4.6 0.9 fusion.51
  5.8 44.6 %all-gather = bf16[32,2,4096]{2,1,0:T(2,128)(2,1)S(1)} all-gather(bf16[1,2,4096]{2,1,0:T(2,128)(2,1)S(1)} %reshape.208), channel_id=1, replica_groups=mesh['grp'=1,'row'=32] {'row'}, dimensions={0}, use_global_device_ids=true | all-gather | bytes 540672 | tf_op jit(solution)/shard_map/all_gather | solution.py:64
  50.9 38.1 %all-gather.1 = bf16[32,2,4096]{2,1,0:T(2,128)(2,1)S(1)} all-gather(bf16[1,2,4096]{2,1,0:T(2,128)(2,1)S(1)} %reshape.210), channel_id=1, replica_groups=mesh['grp'=1,'row'=32] {'row'}, dimensions={0}, use_global_device_ids=true | all-gather | bytes 540672 | tf_op jit(solution)/shard_map/all_gather | solution.py:65
  89.7 4.5 %convert_element_type.106 = bf16[4,32,128,32]{3,2,1,0:T(8,128)(2,1)} reshape(bf16[128,4096]{1,0:T(8,128)(2,1)S(1)} %convolution_convert_fusion) | data formatting | bytes 2097152 | tf_op jit(solution)/shard_map/convert_element_type | solution.py:75
  94.1 3.6 %copy.75 = bf16[4,128,32,32]{1,3,2,0:T(8,128)(2,1)S(1)} copy(bf16[4,128,32,32]{3,1,2,0:T(8,128)(2,1)} %bitcast.135) | data formatting | bytes 2097152 | tf_op jit(solution)/shard_map/convert_element_type | solution.py:75
  97.7 37.9 %all-gather.2 = bf16[32,2,128]{2,1,0:T(2,128)(2,1)S(1)} all-gather(bf16[1,2,128]{2,1,0:T(2,128)(2,1)S(1)} %get-tuple-element.101), channel_id=1, replica_groups=mesh['grp'=1,'row'=32] {'row'}, dimensions={0}, use_global_device_ids=true | all-gather | bytes 16896 | tf_op jit(solution)/shard_map/all_gather | solution.py:66
  136.1 0.5 convolution_divide_fusion
  136.6 0.5 fusion.63
  138.0 0.8 copy.83
  138.8 2.6 %all-to-all-start = ((bf16[128,4,128]{2,1,0:T(4,128)(2,1)}), bf16[128,4,128]{2,1,0:T(4,128)(2,1)S(1)}, u32[]{:S(2)}, u32[]{:S(2)}) async-start(bf16[128,4,128]{2,1,0:T(4,128)(2,1)} %bitcast.22), calls=%async_computation | async-start | bytes 262144 | tf_op jit(solution)/shard_map/all_to_all | solution.py:118
  141.9 42.5 %all_gather.15 = bf16[8,128,128]{2,0,1:T(8,128)(2,1)S(1)} all-gather(bf16[8,4,128]{2,0,1:T(8,128)(2,1)S(1)} %fusion.35), channel_id=1, replica_groups=mesh['grp'=1,'row'=32] {'row'}, dimensions={1}, use_global_device_ids=true | all-gather | bytes 270336 | tf_op jit(solution)/shard_map/all_gather | solution.py:106
  184.4 0.8 copy.86
  186.1 2.6 %all-to-all-start.1 = ((bf16[128,4,128]{2,1,0:T(4,128)(2,1)}), bf16[128,4,128]{2,1,0:T(4,128)(2,1)S(1)}, u32[]{:S(2)}, u32[]{:S(2)}) async-start(bf16[128,4,128]{2,1,0:T(4,128)(2,1)} %bitcast.27), calls=%async_computation.1 | async-start | bytes 262144 | tf_op jit(solution)/shard_map/all_to_all | solution.py:119
  188.8 2.0 while.10
  190.9 6.1 %all-to-all-done.1 = bf16[128,4,128]{2,1,0:T(4,128)(2,1)S(1)} async-done(((bf16[128,4,128]{2,1,0:T(4,128)(2,1)}), bf16[128,4,128]{2,1,0:T(4,128)(2,1)S(1)}, u32[]{:S(2)}, u32[]{:S(2)}) %all-to-all-start.1) | async-done | bytes 131104 | tf_op jit(solution)/shard_map/all_to_all | solution.py:119
  197.3 0.8 copy.90
  198.1 2.6 %all-to-all-start.2 = ((bf16[4,128,128]{2,0,1:T(4,128)(2,1)}), bf16[4,128,128]{2,0,1:T(4,128)(2,1)S(1)}, u32[]{:S(2)}, u32[]{:S(2)}) async-start(bf16[4,128,128]{2,0,1:T(4,128)(2,1)} %copy.90), calls=%async_computation.2 | async-start | bytes 262144 | tf_op jit(solution)/shard_map/all_to_all | solution.py:124
  201.1 0.9 fusion.33
  202.0 6.9 %all-to-all-done.2 = bf16[4,128,128]{2,0,1:T(4,128)(2,1)S(1)} async-done(((bf16[4,128,128]{2,0,1:T(4,128)(2,1)}), bf16[4,128,128]{2,0,1:T(4,128)(2,1)S(1)}, u32[]{:S(2)}, u32[]{:S(2)}) %all-to-all-start.2) | async-done | bytes 131104 | tf_op jit(solution)/shard_map/all_to_all | solution.py:124
  209.2 0.8 fusion.34
  (87 shorter events, 7.2 us)
Async XLA Ops:
  0.6 140.9 %copy-start = (bf16[256,1024]{1,0:T(8,128)(2,1)S(1)}, bf16[256,1024]{1,0:T(8,128)(2,1)}, u32[]{:S(2)}) copy-start(bf16[256,1024]{1,0:T(8,128)(2,1)} %param.24) | copy-start | bytes 1572868
  89.6 46.2 %copy-start.10 = (s32[128]{0:T(128)S(1)}, s32[128]{0:T(128)}, u32[]{:S(2)}) copy-start(s32[128]{0:T(128)} %param.19) | copy-start | bytes 1540
  89.6 46.3 %copy-start.9 = (s32[128]{0:T(128)S(1)}, s32[128]{0:T(128)}, u32[]{:S(2)}) copy-start(s32[128]{0:T(128)} %param.20) | copy-start | bytes 1540
  89.6 46.4 %copy-start.11 = (bf16[1024,128]{1,0:T(8,128)(2,1)S(1)}, bf16[1024,128]{1,0:T(8,128)(2,1)}, u32[]{:S(2)}) copy-start(bf16[1024,128]{1,0:T(8,128)(2,1)} %param.23) | copy-start | bytes 786436
  94.1 42.5 %copy-start.3 = (bf16[4,128,128]{2,1,0:T(8,128)(2,1)S(1)}, bf16[4,128,128]{2,1,0:T(8,128)(2,1)}, u32[]{:S(2)}) copy-start(bf16[4,128,128]{2,1,0:T(8,128)(2,1)} %param.18) | copy-start | bytes 393220
  94.1 42.5 %copy-start.5 = (f32[66,128]{1,0:T(8,128)S(1)}, f32[66,128]{1,0:T(8,128)}, u32[]{:S(2)}) copy-start(f32[66,128]{1,0:T(8,128)} %param.21) | copy-start | bytes 101380
  94.1 43.4 %copy-start.2 = (bf16[128,512]{1,0:T(8,128)(2,1)S(1)}, bf16[128,512]{1,0:T(8,128)(2,1)}, u32[]{:S(2)}) copy-start(bf16[128,512]{1,0:T(8,128)(2,1)} %param.27) | copy-start | bytes 393220
  97.7 43.7 %copy-start.8 = (bf16[128,8]{0,1:T(8,128)(2,1)S(1)}, bf16[128,8]{0,1:T(8,128)(2,1)}, u32[]{:S(2)}) copy-start(bf16[128,8]{0,1:T(8,128)(2,1)} %param.26) | copy-start | bytes 6148
  137.8 48.3 %copy-start.7 = (s32[2,128]{1,0:T(2,128)S(1)}, s32[2,128]{1,0:T(2,128)}, u32[]{:S(2)}) copy-start(s32[2,128]{1,0:T(2,128)} %param.17) | copy-start | bytes 3076
  138.8 47.3 %all-to-all-start = ((bf16[128,4,128]{2,1,0:T(4,128)(2,1)}), bf16[128,4,128]{2,1,0:T(4,128)(2,1)S(1)}, u32[]{:S(2)}, u32[]{:S(2)}) async-start(bf16[128,4,128]{2,1,0:T(4,128)(2,1)} %bitcast.22), calls=%async_computation | async-start | bytes 262144 | tf_op jit(solution)/shard_map/all_to_all | solution.py:118
  186.1 10.8 %all-to-all-start.1 = ((bf16[128,4,128]{2,1,0:T(4,128)(2,1)}), bf16[128,4,128]{2,1,0:T(4,128)(2,1)S(1)}, u32[]{:S(2)}, u32[]{:S(2)}) async-start(bf16[128,4,128]{2,1,0:T(4,128)(2,1)} %bitcast.27), calls=%async_computation.1 | async-start | bytes 262144 | tf_op jit(solution)/shard_map/all_to_all | solution.py:119
  188.7 11.9 %copy-start.12 = (bf16[128,128]{1,0:T(8,128)(2,1)S(1)}, bf16[128,128]{1,0:T(8,128)(2,1)}, u32[]{:S(2)}) copy-start(bf16[128,128]{1,0:T(8,128)(2,1)} %param.28) | copy-start | bytes 98308
  188.8 12.3 %copy-start.1 = (bf16[2,128,256]{2,1,0:T(8,128)(2,1)S(1)}, bf16[2,128,256]{2,1,0:T(8,128)(2,1)}, u32[]{:S(2)}) copy-start(bf16[2,128,256]{2,1,0:T(8,128)(2,1)} %param.16) | copy-start | bytes 393220
  188.8 12.3 %copy-start.4 = (bf16[256,256]{1,0:T(8,128)(2,1)S(1)}, bf16[256,256]{1,0:T(8,128)(2,1)}, u32[]{:S(2)}) copy-start(bf16[256,256]{1,0:T(8,128)(2,1)} %param.25) | copy-start | bytes 393220
  190.8 18.5 %copy-start.6 = (bf16[128,128]{1,0:T(8,128)(2,1)S(1)}, bf16[128,128]{1,0:T(8,128)(2,1)}, u32[]{:S(2)}) copy-start(bf16[128,128]{1,0:T(8,128)(2,1)} %param.29) | copy-start | bytes 98308
  198.1 10.8 %all-to-all-start.2 = ((bf16[4,128,128]{2,0,1:T(4,128)(2,1)}), bf16[4,128,128]{2,0,1:T(4,128)(2,1)S(1)}, u32[]{:S(2)}, u32[]{:S(2)}) async-start(bf16[4,128,128]{2,0,1:T(4,128)(2,1)} %copy.90), calls=%async_computation.2 | async-start | bytes 262144 | tf_op jit(solution)/shard_map/all_to_all | solution.py:124
where the time goes:
time: 211 us; the launch traced here: 210 us
  blocking collectives  163 us (77%)
  local copies, waits for them, and re-layouts  13 us (6%)
  waiting for transfers between devices  13 us (6%)
  starting transfers between devices  7.74 us (4%)
  matrix products  7.36 us (3%)
  other arithmetic  4.76 us (2%)
    all_gather x1, blocking collectives, on_device(): lax.all_gather(left_factor, 'row', axis=0, tiled=True)  44.6 us
    all_gather x1, blocking collectives, on_device(): full_bias = lax.all_gather(head_bias, 'row', axis=1, tiled=True)  42.5 us
    all_gather x1, blocking collectives, on_device(): lax.all_gather(right_factor, 'row', axis=0, tiled=True)  38.1 us
    all_gather x1, blocking collectives, on_device(): lax.all_gather(live_weights, 'row', axis=0, tiled=True)  37.9 us
    convert_element_type x2, local copies, waits for them, and re-layouts, on_device(): outer_flat.reshape(res_local * residue_total, opm_width * opm_width)  8.06 us
    all_to_all x1, waiting for transfers between devices, on_device(): lax.all_to_all(channel_sum, 'row', split_axis=1, concat_axis=0, tiled=True)  6.94 us
    all_to_all x1, waiting for transfers between devices, on_device(): lax.all_to_all(tri_right, 'row', split_axis=0, concat_axis=1, tiled=True)  6.06 us
  transfers between devices with their start and end apart: 3, of which 2 were waited for; matrix products, arithmetic and copies ran while one was open for 3% of the time, Pallas kernels for 0%

commit v1 on v0

--- a/solution.py
+++ b/solution.py
@@ -1,9 +1,26 @@
+import functools
 import jax
 import jax.numpy as jnp
 from jax import lax
 from jax.sharding import PartitionSpec as P
 
 REL_MAX = 32
+
+
+def attach_roads_in(load, device_axis):
+    block_out = lax.axis_index(device_axis)
+    main = lax.axis_size(device_axis)
+    t1, local_out, t_next = (main, block_out, load.shape[0])
+    f_now, n_now = (load, 1)
+    while n_now < t1:
+        passed = lax.ppermute(f_now, device_axis, [(w, (w - n_now) % t1) for w in range(t1)])
+        f_now = jnp.concatenate([f_now, passed], 0)
+        n_now = 2 * n_now
+    earlier = jnp.roll(f_now, local_out * t_next, 0)
+    return earlier
+
+
+_finish_surface = functools.partial(attach_roads_in, device_axis="row")
 
 
 def layer_normalize(values):
@@ -62,7 +79,7 @@
     live_weights = active_entry_mask.astype(jnp.bfloat16)
     left_all, right_all, live_all = (
         lax.all_gather(left_factor, "row", axis=0, tiled=True),
-        lax.all_gather(right_factor, "row", axis=0, tiled=True),
+        _finish_surface(right_factor),
         lax.all_gather(live_weights, "row", axis=0, tiled=True),
     )
     left_cols = lax.dynamic_slice_in_dim(left_all, row_start * opm_width, res_local * opm_width, 1)

time: 211 us -> 199 us (0.943)
  blocking collectives: 163 us -> 121 us
  waiting for transfers between devices: 13 us -> 31.2 us
  starting transfers between devices: 7.74 us -> 15.3 us
  local copies, waits for them, and re-layouts: 13 us -> 15.9 us
    all_gather x1 -> x0, blocking collectives: 38.1 us -> none  [on_device(): lax.all_gather(right_factor, 'row', axis=0, tiled=True)]
    ppermute x0 -> x5, waiting for transfers between devices: none -> 18.2 us  [attach_roads_in(): lax.ppermute(f_now, device_axis, [(w, (w - n_now) % t1) for w in range(t1)])]
    ppermute x0 -> x5, starting transfers between devices: none -> 7.23 us  [attach_roads_in(): lax.ppermute(f_now, device_axis, [(w, (w - n_now) % t1) for w in range(t1)])]
  transfers between devices with their start and end apart: 3 -> 8, of which waited for: 2 -> 5; matrix products, arithmetic and copies ran while one was open for 3% -> 5% of each run, Pallas kernels for 0% -> 0%
where the time goes in v1:
time: 199 us
  blocking collectives  121 us (61%)
  waiting for transfers between devices  31.2 us (16%)
  local copies, waits for them, and re-layouts  15.9 us (8%)
  starting transfers between devices  15.3 us (8%)
  matrix products  8.05 us (4%)
  other arithmetic  5.62 us (3%)
    all_gather x1, blocking collectives, on_device(): lax.all_gather(left_factor, 'row', axis=0, tiled=True)  42.6 us
    all_gather x1, blocking collectives, on_device(): full_bias = lax.all_gather(head_bias, 'row', axis=1, tiled=True)  42.5 us
    all_gather x1, blocking collectives, on_device(): lax.all_gather(live_weights, 'row', axis=0, tiled=True)  36.4 us
    ppermute x5, waiting for transfers between devices, attach_roads_in(): lax.ppermute(f_now, device_axis, [(w, (w - n_now) % t1) for w in range(t1)])  18.2 us
    convert_element_type x2, local copies, waits for them, and re-layouts, on_device(): outer_flat.reshape(res_local * residue_total, opm_width * opm_width)  8.04 us
    ppermute x5, starting transfers between devices, attach_roads_in(): lax.ppermute(f_now, device_axis, [(w, (w - n_now) % t1) for w in range(t1)])  7.23 us
    all_to_all x1, waiting for transfers between devices, on_device(): lax.all_to_all(channel_sum, 'row', split_axis=1, concat_axis=0, tiled=True)  6.94 us
    all_to_all x1, waiting for transfers between devices, on_device(): lax.all_to_all(tri_right, 'row', split_axis=0, concat_axis=1, tiled=True)  6.07 us
  transfers between devices with their start and end apart: 8, of which 5 were waited for; matrix products, arithmetic and copies ran while one was open for 5% of the time, Pallas kernels for 0%

profile of v1, /device:TPU:0, one launch (start us, length us, event | category | flops | bytes accessed | tf_op | source)
XLA Modules:
  0.0 198.8 jit_solution(2463338795604930226)
XLA Ops:
  0.6 1.1 convert_reduce_fusion
  1.7 1.1 multiply_reduce_fusion.2
  2.8 1.0 multiply_convert_fusion.2
  4.6 0.9 fusion.52
  5.8 6.4 %collective-permute-start = (bf16[2,4096]{1,0:T(2,128)(2,1)S(1)}, bf16[2,4096]{1,0:T(2,128)(2,1)S(1)}, u32[]{:S(2)}, u32[]{:S(2)}) collective-permute-start(bf16[2,4096]{1,0:T(2,128)(2,1)S(1)} %reshape.194), channel_id=1, source_target_pairs={{0,31},{1,0},{2,1},{3,2},{4,3},{5,4},{6,5},{7,6},{8,7},{9,8},{10,9... | collective-permute-start | bytes 49160 | tf_op jit(solution)/shard_map/ppermute | solution.py:16
  12.5 1.2 collective-permute-done
  14.3 42.6 %all-gather = bf16[32,2,4096]{2,1,0:T(2,128)(2,1)S(1)} all-gather(bf16[1,2,4096]{2,1,0:T(2,128)(2,1)S(1)} %reshape.208), channel_id=1, replica_groups=mesh['grp'=1,'row'=32] {'row'}, dimensions={0}, use_global_device_ids=true | all-gather | bytes 540672 | tf_op jit(solution)/shard_map/all_gather | solution.py:81
  58.8 36.4 %all-gather.1 = bf16[32,2,128]{2,1,0:T(2,128)(2,1)S(1)} all-gather(bf16[1,2,128]{2,1,0:T(2,128)(2,1)S(1)} %get-tuple-element.101), channel_id=1, replica_groups=mesh['grp'=1,'row'=32] {'row'}, dimensions={0}, use_global_device_ids=true | all-gather | bytes 16896 | tf_op jit(solution)/shard_map/all_gather | solution.py:83
  95.6 5.4 %collective-permute-done.3 = bf16[16,4096]{1,0:T(8,128)(2,1)S(1)} collective-permute-done((bf16[16,4096]{1,0:T(8,128)(2,1)S(1)}, bf16[16,4096]{1,0:T(8,128)(2,1)S(1)}, u32[]{:S(2)}, u32[]{:S(2)}) %collective-permute-start.3) | collective-permute-done | bytes 131104 | tf_op jit(solution)/shard_map/ppermute | solution.py:16
  102.0 1.0 reshape.209
  103.7 11.5 %collective-permute-done.4 = bf16[32,4096]{1,0:T(8,128)(2,1)S(1)} collective-permute-done((bf16[32,4096]{1,0:T(8,128)(2,1)S(1)}, bf16[32,4096]{1,0:T(8,128)(2,1)S(1)}, u32[]{:S(2)}, u32[]{:S(2)}) %collective-permute-start.4) | collective-permute-done | bytes 262176 | tf_op jit(solution)/shard_map/ppermute | solution.py:16
  115.6 1.2 convolution_convert_fusion
  116.8 4.4 %convert_element_type.106 = bf16[4,32,128,32]{3,2,1,0:T(8,128)(2,1)} reshape(bf16[128,4096]{1,0:T(8,128)(2,1)S(1)} %convolution_convert_fusion) | data formatting | bytes 2097152 | tf_op jit(solution)/shard_map/convert_element_type | solution.py:92
  121.2 3.6 %copy.75 = bf16[4,128,32,32]{1,3,2,0:T(8,128)(2,1)S(1)} copy(bf16[4,128,32,32]{3,1,2,0:T(8,128)(2,1)} %bitcast.134) | data formatting | bytes 2097152 | tf_op jit(solution)/shard_map/convert_element_type | solution.py:92
  126.8 0.8 copy.83
  127.5 2.9 %all-to-all-start = ((bf16[128,4,128]{2,1,0:T(4,128)(2,1)}), bf16[128,4,128]{2,1,0:T(4,128)(2,1)S(1)}, u32[]{:S(2)}, u32[]{:S(2)}) async-start(bf16[128,4,128]{2,1,0:T(4,128)(2,1)} %bitcast.22), calls=%async_computation | async-start | bytes 262144 | tf_op jit(solution)/shard_map/all_to_all | solution.py:135
  132.1 42.5 %all_gather.11 = bf16[8,128,128]{2,0,1:T(8,128)(2,1)S(1)} all-gather(bf16[8,4,128]{2,0,1:T(8,128)(2,1)S(1)} %fusion.35), channel_id=1, replica_groups=mesh['grp'=1,'row'=32] {'row'}, dimensions={1}, use_global_device_ids=true | all-gather | bytes 270336 | tf_op jit(solution)/shard_map/all_gather | solution.py:123
  174.8 2.6 %all-to-all-start.1 = ((bf16[128,4,128]{2,1,0:T(4,128)(2,1)}), bf16[128,4,128]{2,1,0:T(4,128)(2,1)S(1)}, u32[]{:S(2)}, u32[]{:S(2)}) async-start(bf16[128,4,128]{2,1,0:T(4,128)(2,1)} %bitcast.27), calls=%async_computation.1 | async-start | bytes 262144 | tf_op jit(solution)/shard_map/all_to_all | solution.py:136
  177.5 2.0 while.10
  179.6 6.1 %all-to-all-done.1 = bf16[128,4,128]{2,1,0:T(4,128)(2,1)S(1)} async-done(((bf16[128,4,128]{2,1,0:T(4,128)(2,1)}), bf16[128,4,128]{2,1,0:T(4,128)(2,1)S(1)}, u32[]{:S(2)}, u32[]{:S(2)}) %all-to-all-start.1) | async-done | bytes 131104 | tf_op jit(solution)/shard_map/all_to_all | solution.py:136
  186.8 2.6 %all-to-all-start.2 = ((bf16[4,128,128]{2,0,1:T(4,128)(2,1)}), bf16[4,128,128]{2,0,1:T(4,128)(2,1)S(1)}, u32[]{:S(2)}, u32[]{:S(2)}) async-start(bf16[4,128,128]{2,0,1:T(4,128)(2,1)} %copy.90), calls=%async_computation.2 | async-start | bytes 262144 | tf_op jit(solution)/shard_map/all_to_all | solution.py:141
  189.8 0.9 fusion.33
  190.7 6.9 %all-to-all-done.2 = bf16[4,128,128]{2,0,1:T(4,128)(2,1)S(1)} async-done(((bf16[4,128,128]{2,0,1:T(4,128)(2,1)}), bf16[4,128,128]{2,0,1:T(4,128)(2,1)S(1)}, u32[]{:S(2)}, u32[]{:S(2)}) %all-to-all-start.2) | async-done | bytes 131104 | tf_op jit(solution)/shard_map/all_to_all | solution.py:141
  198.0 0.8 fusion.34
  (98 shorter events, 13.6 us)
Async XLA Ops:
  0.6 56.4 %copy-start = (bf16[256,1024]{1,0:T(8,128)(2,1)S(1)}, bf16[256,1024]{1,0:T(8,128)(2,1)}, u32[]{:S(2)}) copy-start(bf16[256,1024]{1,0:T(8,128)(2,1)} %param.24) | copy-start | bytes 1572868
  5.8 7.9 %collective-permute-start = (bf16[2,4096]{1,0:T(2,128)(2,1)S(1)}, bf16[2,4096]{1,0:T(2,128)(2,1)S(1)}, u32[]{:S(2)}, u32[]{:S(2)}) collective-permute-start(bf16[2,4096]{1,0:T(2,128)(2,1)S(1)} %reshape.194), channel_id=1, source_target_pairs={{0,31},{1,0},{2,1},{3,2},{4,3},{5,4},{6,5},{7,6},{8,7},{9,8},{10,9... | collective-permute-start | bytes 49160 | tf_op jit(solution)/shard_map/ppermute | solution.py:16
  13.7 43.2 %collective-permute-start.1 = (bf16[4,4096]{1,0:T(4,128)(2,1)S(1)}, bf16[4,4096]{1,0:T(4,128)(2,1)S(1)}, u32[]{:S(2)}, u32[]{:S(2)}) collective-permute-start(bf16[4,4096]{1,0:T(4,128)(2,1)S(1)} %pad_maximum_fusion.2), channel_id=1, source_target_pairs={{0,30},{1,31},{2,0},{3,1},{4,2},{5,3},{6,4},{7,5},{8,6},{9,7},{10,... | collective-permute-start | bytes 98312 | tf_op jit(solution)/shard_map/ppermute | solution.py:16
  56.9 38.3 %collective-permute-start.2 = (bf16[8,4096]{1,0:T(8,128)(2,1)S(1)}, bf16[8,4096]{1,0:T(8,128)(2,1)S(1)}, u32[]{:S(2)}, u32[]{:S(2)}) collective-permute-start(bf16[8,4096]{1,0:T(8,128)(2,1)S(1)} %pad_maximum_fusion.1), channel_id=1, source_target_pairs={{0,28},{1,29},{2,30},{3,31},{4,0},{5,1},{6,2},{7,3},{8,4},{9,5},{1... | collective-permute-start | bytes 196616 | tf_op jit(solution)/shard_map/ppermute | solution.py:16
  95.3 5.8 %collective-permute-start.3 = (bf16[16,4096]{1,0:T(8,128)(2,1)S(1)}, bf16[16,4096]{1,0:T(8,128)(2,1)S(1)}, u32[]{:S(2)}, u32[]{:S(2)}) collective-permute-start(bf16[16,4096]{1,0:T(8,128)(2,1)S(1)} %pad_maximum_fusion), channel_id=1, source_target_pairs={{0,24},{1,25},{2,26},{3,27},{4,28},{5,29},{6,30},{7,31},{8,0},{9,1... | collective-permute-start | bytes 393224 | tf_op jit(solution)/shard_map/ppermute | solution.py:16
  101.2 14.1 %collective-permute-start.4 = (bf16[32,4096]{1,0:T(8,128)(2,1)S(1)}, bf16[32,4096]{1,0:T(8,128)(2,1)S(1)}, u32[]{:S(2)}, u32[]{:S(2)}) collective-permute-start(bf16[32,4096]{1,0:T(8,128)(2,1)S(1)} %concatenate.25), channel_id=1, source_target_pairs={{0,16},{1,17},{2,18},{3,19},{4,20},{5,21},{6,22},{7,23},{8,24},{9,... | collective-permute-start | bytes 786440 | tf_op jit(solution)/shard_map/ppermute | solution.py:16
  116.7 8.1 %copy-start.10 = (bf16[1024,128]{1,0:T(8,128)(2,1)S(1)}, bf16[1024,128]{1,0:T(8,128)(2,1)}, u32[]{:S(2)}) copy-start(bf16[1024,128]{1,0:T(8,128)(2,1)} %param.23) | copy-start | bytes 786436
  121.2 4.1 %copy-start.4 = (bf16[4,128,128]{2,1,0:T(8,128)(2,1)S(1)}, bf16[4,128,128]{2,1,0:T(8,128)(2,1)}, u32[]{:S(2)}) copy-start(bf16[4,128,128]{2,1,0:T(8,128)(2,1)} %param.18) | copy-start | bytes 393220
  121.2 4.2 %copy-start.6 = (f32[66,128]{1,0:T(8,128)S(1)}, f32[66,128]{1,0:T(8,128)}, u32[]{:S(2)}) copy-start(f32[66,128]{1,0:T(8,128)} %param.21) | copy-start | bytes 101380
  121.2 5.1 %copy-start.3 = (bf16[128,512]{1,0:T(8,128)(2,1)S(1)}, bf16[128,512]{1,0:T(8,128)(2,1)}, u32[]{:S(2)}) copy-start(bf16[128,512]{1,0:T(8,128)(2,1)} %param.27) | copy-start | bytes 393220
  124.8 5.7 %copy-start.8 = (s32[2,128]{1,0:T(2,128)S(1)}, s32[2,128]{1,0:T(2,128)}, u32[]{:S(2)}) copy-start(s32[2,128]{1,0:T(2,128)} %param.17) | copy-start | bytes 3076
  124.8 5.7 %copy-start.2 = (bf16[256,256]{1,0:T(8,128)(2,1)S(1)}, bf16[256,256]{1,0:T(8,128)(2,1)}, u32[]{:S(2)}) copy-start(bf16[256,256]{1,0:T(8,128)(2,1)} %get-tuple-element.98) | copy-start | bytes 393220
  125.3 6.7 %copy-start.9 = (bf16[128,8]{0,1:T(8,128)(2,1)S(1)}, bf16[128,8]{0,1:T(8,128)(2,1)}, u32[]{:S(2)}) copy-start(bf16[128,8]{0,1:T(8,128)(2,1)} %param.26) | copy-start | bytes 6148
  127.5 47.3 %all-to-all-start = ((bf16[128,4,128]{2,1,0:T(4,128)(2,1)}), bf16[128,4,128]{2,1,0:T(4,128)(2,1)S(1)}, u32[]{:S(2)}, u32[]{:S(2)}) async-start(bf16[128,4,128]{2,1,0:T(4,128)(2,1)} %bitcast.22), calls=%async_computation | async-start | bytes 262144 | tf_op jit(solution)/shard_map/all_to_all | solution.py:135
  174.8 10.8 %all-to-all-start.1 = ((bf16[128,4,128]{2,1,0:T(4,128)(2,1)}), bf16[128,4,128]{2,1,0:T(4,128)(2,1)S(1)}, u32[]{:S(2)}, u32[]{:S(2)}) async-start(bf16[128,4,128]{2,1,0:T(4,128)(2,1)} %bitcast.27), calls=%async_computation.1 | async-start | bytes 262144 | tf_op jit(solution)/shard_map/all_to_all | solution.py:136
  177.4 12.0 %copy-start.11 = (bf16[128,128]{1,0:T(8,128)(2,1)S(1)}, bf16[128,128]{1,0:T(8,128)(2,1)}, u32[]{:S(2)}) copy-start(bf16[128,128]{1,0:T(8,128)(2,1)} %param.28) | copy-start | bytes 98308
  177.5 12.3 %copy-start.1 = (bf16[2,128,256]{2,1,0:T(8,128)(2,1)S(1)}, bf16[2,128,256]{2,1,0:T(8,128)(2,1)}, u32[]{:S(2)}) copy-start(bf16[2,128,256]{2,1,0:T(8,128)(2,1)} %param.16) | copy-start | bytes 393220
  177.5 12.3 %copy-start.5 = (bf16[256,256]{1,0:T(8,128)(2,1)S(1)}, bf16[256,256]{1,0:T(8,128)(2,1)}, u32[]{:S(2)}) copy-start(bf16[256,256]{1,0:T(8,128)(2,1)} %param.25) | copy-start | bytes 393220
  179.5 18.5 %copy-start.7 = (bf16[128,128]{1,0:T(8,128)(2,1)S(1)}, bf16[128,128]{1,0:T(8,128)(2,1)}, u32[]{:S(2)}) copy-start(bf16[128,128]{1,0:T(8,128)(2,1)} %param.29) | copy-start | bytes 98308
  186.8 10.8 %all-to-all-start.2 = ((bf16[4,128,128]{2,0,1:T(4,128)(2,1)}), bf16[4,128,128]{2,0,1:T(4,128)(2,1)S(1)}, u32[]{:S(2)}, u32[]{:S(2)}) async-start(bf16[4,128,128]{2,0,1:T(4,128)(2,1)} %copy.90), calls=%async_computation.2 | async-start | bytes 262144 | tf_op jit(solution)/shard_map/all_to_all | solution.py:141
